TPU v7x, 256 devices: a whole 4x4x8 slice. The times are simulated.
256 devices in a mesh: row: 8 (over x_hi, y), col: 32 (over z, x_lo, core).
Axes of the slice: x: 4 (x_hi: 2, x_lo: 2; x = x_hi * 2 + x_lo), y: 4, z: 8, core: 2. Of those that a mesh axis runs over, the one named last changes fastest.
Arguments:
- samples: float32 [1024, 64, 128], P(('row', 'col')), may hold values from -6 to 6
- omega: float32 [8, 32, 100, 128, 128], P('row', 'col'), may hold values from -0.12 to 2.12
- block_rows: int32 [8, 32, 100], P('row', 'col'), may hold values from -1 to 1023, as said below
- block_cols: int32 [8, 32, 100], P('row', 'col'), may hold values from -1 to 1023, as said below
Outputs:
- omega_next: float32 [8, 32, 100, 128, 128], P('row', 'col')
Inputs may be any that keep to these rules, and one draw needn't show every extreme that they name: `block_rows`: slots 0 to 3 of the device at (a, b) hold the diagonal blocks I = J = (a * 32 + b) * 4 + k in order of k; the other slots hold distinct off-diagonal blocks whose block row lies in a * 1024 / 8 up to (a + 1) * 1024 / 8 - 1 and whose block column J has (J // 4) % 32 = b; live slots come first and -1 fills the rest; some device has all 100 slots live. `block_cols`: -1 exactly where block_rows is -1.
All inputs are finite; a program needn't handle non-finite values.
Results may differ from a plain program's by a relative error of at most 0.0003.
Values sent between devices are 32-bit elements; how exact they have to be, the bound alone decides.
A program may use at most 128 MiB of HBM per device.

v0:
```python
import jax
import jax.numpy as jnp
from jax import lax
from jax.sharding import PartitionSpec as P

ITERS = 2
STEP = 0.5
PENALTY = 0.1


def gradient_blocks(left_totals, right_samples, left_samples, right_totals, sample_count):
    forward = jnp.einsum(
        "snb,snk->sbk", left_totals, right_samples, precision=lax.Precision.HIGHEST
    )
    mirrored = jnp.einsum(
        "snb,snk->sbk", left_samples, right_totals, precision=lax.Precision.HIGHEST
    )
    return (forward + mirrored) * (0.5 / sample_count)


def proximal(current, grad, active, on_diagonal):
    stepped = current - STEP * grad
    eye_mask = jnp.eye(current.shape[-1], dtype=bool)[None] & on_diagonal[:, None, None]
    shrunk = jnp.sign(stepped) * jnp.maximum(jnp.abs(stepped) - STEP * PENALTY, 0.0)
    lifted = 0.5 * (stepped + jnp.sqrt(stepped * stepped + 4.0 * STEP))
    updated = jnp.where(eye_mask, lifted, shrunk)
    return jnp.where(active[:, None, None], updated, 0.0)


def shards(samples, omega, block_rows, block_cols):
    col_count = lax.axis_size("col")
    row_index = lax.axis_index("row")
    slab_blocks = samples.shape[0]
    sample_count = samples.shape[1]
    width = samples.shape[2]
    group_rows = slab_blocks * col_count
    current = omega[0, 0]
    row_ids = block_rows[0, 0]
    col_ids = block_cols[0, 0]
    active = row_ids >= 0
    local_rows = jnp.where(active, row_ids - row_index * group_rows, -1)
    safe_rows = jnp.maximum(local_rows, 0)
    slab_ids = col_ids // slab_blocks
    local_cols = jnp.where(active, slab_ids // col_count * slab_blocks + col_ids % slab_blocks, 0)
    on_diagonal = active & (row_ids == col_ids)
    row_samples = lax.all_gather(samples, "col", axis=0, tiled=True)
    col_samples = lax.all_gather(samples, "row", axis=0, tiled=True)
    picked_cols = col_samples[local_cols]
    picked_rows = row_samples[safe_rows]
    for iteration in range(ITERS):
        products = jnp.einsum("snk,sbk->snb", picked_cols, current, precision=lax.Precision.HIGHEST)
        flattened = products.reshape(products.shape[0], -1)

        def rows_term(offset, length, flattened=flattened):
            selector = (local_rows[None, :] == jnp.arange(length)[:, None]).astype(jnp.float32)
            summed_part = jnp.dot(selector, flattened, precision=lax.Precision.HIGHEST)
            return summed_part.reshape(length, sample_count, width)

        own_totals = lax.psum_scatter(
            rows_term(jnp.int32(0), slab_blocks * lax.axis_size("col")),
            "col",
            scatter_dimension=0,
            tiled=True,
        )
        row_totals = lax.all_gather(own_totals, "col", axis=0, tiled=True)
        col_totals = lax.all_gather(own_totals, "row", axis=0, tiled=True)
        grad = gradient_blocks(
            row_totals[safe_rows], picked_cols, picked_rows, col_totals[local_cols], sample_count
        )
        current = proximal(current, grad, active, on_diagonal)
    return current[None, None]


def solution(mesh):
    return jax.shard_map(
        shards,
        mesh=mesh,
        in_specs=(
            P(("row", "col"), None, None),
            P("row", "col", None, None, None),
            P("row", "col", None),
            P("row", "col", None),
        ),
        out_specs=P("row", "col", None, None, None),
        check_vma=False,
    )
```

profile of v0, /device:TPU:1, one launch (start us, length us, event | category | flops | bytes accessed | tf_op | source)
XLA Modules:
  0.0 751.3 jit_solution(15371741248821138310)
XLA Ops:
  6.5 0.7 all-gather.7.cloned.1.call-update
  7.3 0.7 fusion.16
  8.0 0.7 bitcast_select_fusion.2
  8.7 54.9 %all-gather.7.cloned.1.call-done = f32[32,64,128]{2,1,0:T(8,128)} async-done(((f32[4,64,128]{2,1,0:T(8,128)}), f32[32,64,128]{2,1,0:T(8,128)}) %all-gather.7.cloned.1.call-update) | async-done | bytes 1048592 | tf_op jit(solution)/shard_map/all_gather | solution.py:47
  63.6 2.0 gather_fusion
  65.6 14.8 %fusion.3 = f32[100,64,128]{2,1,0:T(8,128)S(1)} fusion(f32[100,64,128]{2,1,0:T(8,128)S(1)} %gather_fusion, f32[1,1,100,128,128]{4,3,2,1,0:T(8,128)} %param.5), kind=kOutput, calls=%fused_computation.12 | convolution fusion | flops 1258291200 | bytes 13107200 | tf_op jit(solution)/shard_map/snk,sbk->snb/dot_general | solution.py:51
  80.4 0.4 slice_bitcast_fusion.1
  80.8 4.1 fusion.7
  84.9 4.4 copy.16
  89.5 0.7 all-gather.11.cloned.1.call-update
  90.2 121.1 %reduce-scatter.3.cloned.1.call-done = f32[4,64,128]{2,1,0:T(8,128)} async-done(((f32[128,64,128]{2,1,0:T(8,128)}), f32[4,64,128]{2,1,0:T(8,128)}) %reduce-scatter.3.cloned.1.call-update) | async-done | bytes 131088 | tf_op jit(solution)/shard_map/reduce_scatter | solution.py:59
  211.4 0.5 all-gather.9.cloned.1.call-update
  212.3 69.6 %all-gather.11.cloned.1.call-done = f32[128,64,128]{2,1,0:T(8,128)} async-done(((f32[4,64,128]{2,1,0:T(8,128)}), f32[128,64,128]{2,1,0:T(8,128)}) %all-gather.11.cloned.1.call-update) | async-done | bytes 4194320 | tf_op jit(solution)/shard_map/all_gather | solution.py:46
  281.8 4.6 gather_fusion.2
  286.4 47.3 %all-gather.13.cloned.1.call-done = f32[32,64,128]{2,1,0:T(8,128)} async-done(((f32[4,64,128]{2,1,0:T(8,128)}), f32[32,64,128]{2,1,0:T(8,128)}) %all-gather.13.cloned.1.call-update) | async-done | bytes 1048592 | tf_op jit(solution)/shard_map/all_gather | solution.py:66
  333.7 3.6 gather_fusion.3
  337.3 65.5 %all-gather.9.cloned.1.call-done = f32[128,64,128]{2,1,0:T(8,128)} async-done(((f32[4,64,128]{2,1,0:T(8,128)}), f32[128,64,128]{2,1,0:T(8,128)}) %all-gather.9.cloned.1.call-update) | async-done | bytes 4194320 | tf_op jit(solution)/shard_map/all_gather | solution.py:65
  402.8 4.7 gather_fusion.1
  407.5 12.5 %fusion.19 = f32[100,128,128]{2,1,0:T(8,128)S(1)} fusion(f32[100,64,128]{2,1,0:T(8,128)} %gather_fusion.1, f32[100,64,128]{2,1,0:T(8,128)S(1)} %gather_fusion), kind=kOutput, calls=%fused_computation.48 | convolution fusion | flops 1258291200 | bytes 13107200 | tf_op jit(solution)/shard_map/snb,snk->sbk/dot_general | solution.py:12
  420.0 19.4 %fusion = f32[100,128,128]{2,1,0:T(8,128)S(1)} fusion(f32[1,1,100,128,128]{4,3,2,1,0:T(8,128)} %param.5, f32[100,128,128]{2,1,0:T(8,128)S(1)} %fusion.19, pred[100]{0:T(512)(128)(4,1)S(1)} %fusion.18, pred[128,128]{1,0:T(8,128)(4,1)S(1)} %iota_compare_fusion, pred[100]{0:T(512)(128)(4,1)S(1)} %bitcast_and_fusion, f32[100,64,128]{2,1,0:T(8,128)S(1)} %copy-done.1, ...), kind=kOutput, calls=%fused_computation.8 | convolution fusion | flops 1282867200 | bytes 26230984 | tf_op jit(solution)/shard_map/snb,snk->sbk/dot_general | solution.py:15
  439.4 13.0 %fusion.20 = f32[100,64,128]{2,1,0:T(8,128)S(1)} fusion(f32[100,64,128]{2,1,0:T(8,128)S(1)} %gather_fusion, f32[100,128,128]{2,1,0:T(8,128)S(1)} %fusion), kind=kOutput, calls=%fused_computation.49 | convolution fusion | flops 1258291200 | bytes 13107200 | tf_op jit(solution)/shard_map/snk,sbk->snb/dot_general | solution.py:51
  452.3 0.4 slice_bitcast_fusion
  452.8 4.1 fusion.5
  456.9 4.7 copy.18
  461.7 121.0 %reduce-scatter.5.cloned.1.call-done = f32[4,64,128]{2,1,0:T(8,128)} async-done(((f32[128,64,128]{2,1,0:T(8,128)}), f32[4,64,128]{2,1,0:T(8,128)}) %reduce-scatter.5.cloned.1.call-update) | async-done | bytes 131088 | tf_op jit(solution)/shard_map/reduce_scatter | solution.py:59
  582.7 0.7 all-gather.15.cloned.1.call-update
  583.4 53.3 %all-gather.17.cloned.1.call-done = f32[32,64,128]{2,1,0:T(8,128)} async-done(((f32[4,64,128]{2,1,0:T(8,128)}), f32[32,64,128]{2,1,0:T(8,128)}) %all-gather.17.cloned.1.call-update) | async-done | bytes 1048592 | tf_op jit(solution)/shard_map/all_gather | solution.py:66
  636.8 3.7 gather_fusion.5
  640.5 65.5 %all-gather.15.cloned.1.call-done = f32[128,64,128]{2,1,0:T(8,128)} async-done(((f32[4,64,128]{2,1,0:T(8,128)}), f32[128,64,128]{2,1,0:T(8,128)}) %all-gather.15.cloned.1.call-update) | async-done | bytes 4194320 | tf_op jit(solution)/shard_map/all_gather | solution.py:65
  706.0 4.7 gather_fusion.4
  710.7 12.5 %fusion.21 = f32[100,128,128]{2,1,0:T(8,128)S(1)} fusion(f32[100,64,128]{2,1,0:T(8,128)} %gather_fusion.4, f32[100,64,128]{2,1,0:T(8,128)S(1)} %gather_fusion), kind=kOutput, calls=%fused_computation.50 | convolution fusion | flops 1258291200 | bytes 13107200 | tf_op jit(solution)/shard_map/snb,snk->sbk/dot_general | solution.py:12
  723.2 20.7 %fusion.2 = f32[1,1,100,128,128]{4,3,2,1,0:T(8,128)} fusion(f32[100,128,128]{2,1,0:T(8,128)} %copy-done, f32[100,128,128]{2,1,0:T(8,128)S(1)} %fusion.21, pred[100]{0:T(512)(128)(4,1)S(1)} %fusion.18, pred[128,128]{1,0:T(8,128)(4,1)S(1)} %iota_compare_fusion, pred[100]{0:T(512)(128)(4,1)S(1)} %bitcast_and_fusion, f32[100,64,128]{2,1,0:T(8,128)S(1)} %copy-done.2, ...), kind=kOutput, calls=%fused_computation.10 | convolution fusion | flops 1282867200 | bytes 26230984 | tf_op jit(solution)/shard_map/snb,snk->sbk/dot_general | solution.py:15
  (31 shorter events, 0.6 us)
Async XLA Ops:
  6.5 57.0 %all-gather.7.cloned.1.call-start = ((), (), s32[]{:S(2)}) async-start(), calls=%async_computation.2 | async-start | bytes 1179648 | tf_op jit(solution)/shard_map/all_gather | solution.py:47
  7.3 204.1 %reduce-scatter.3.cloned.1.call-start = ((), (), s32[]{:S(2)}) async-start(), calls=%async_computation.3 | async-start | bytes 4325376 | tf_op jit(solution)/shard_map/reduce_scatter | solution.py:59
  89.4 122.9 %copy-start.5 = (s32[1,1,100]{2,1,0:T(1,128)S(1)}, s32[1,1,100]{2,1,0:T(1,128)}, u32[]{:S(2)}) copy-start(s32[1,1,100]{2,1,0:T(1,128)} %param.6) | copy-start | bytes 1204
  89.4 122.9 %copy-start.6 = (s32[1,1,100]{2,1,0:T(1,128)S(1)}, s32[1,1,100]{2,1,0:T(1,128)}, u32[]{:S(2)}) copy-start(s32[1,1,100]{2,1,0:T(1,128)} %param.7) | copy-start | bytes 1204
  89.4 192.4 %all-gather.11.cloned.1.call-start = ((), (), s32[]{:S(2)}) async-start(), calls=%async_computation.5 | async-start | bytes 4325376 | tf_op jit(solution)/shard_map/all_gather | solution.py:46
  90.1 243.6 %all-gather.13.cloned.1.call-start = ((), (), s32[]{:S(2)}) async-start(), calls=%async_computation.6 | async-start | bytes 1179648 | tf_op jit(solution)/shard_map/all_gather | solution.py:66
  211.3 191.4 %all-gather.9.cloned.1.call-start = ((), (), s32[]{:S(2)}) async-start(), calls=%async_computation.4 | async-start | bytes 4325376 | tf_op jit(solution)/shard_map/all_gather | solution.py:65
  211.9 370.7 %reduce-scatter.5.cloned.1.call-start = ((), (), s32[]{:S(2)}) async-start(), calls=%async_computation.7 | async-start | bytes 4325376 | tf_op jit(solution)/shard_map/reduce_scatter | solution.py:59
  407.5 12.5 %copy-start.1 = (f32[100,64,128]{2,1,0:T(8,128)S(1)}, f32[100,64,128]{2,1,0:T(8,128)}, u32[]{:S(2)}) copy-start(f32[100,64,128]{2,1,0:T(8,128)} %gather_fusion.2) | copy-start | bytes 9830404
  407.5 12.5 %copy-start.4 = (f32[100,64,128]{2,1,0:T(8,128)S(1)}, f32[100,64,128]{2,1,0:T(8,128)}, u32[]{:S(2)}) copy-start(f32[100,64,128]{2,1,0:T(8,128)} %gather_fusion.3) | copy-start | bytes 9830404
  439.4 13.0 %copy-start = (f32[100,128,128]{2,1,0:T(8,128)}, f32[100,128,128]{2,1,0:T(8,128)S(1)}, u32[]{:S(2)}) copy-start(f32[100,128,128]{2,1,0:T(8,128)S(1)} %fusion) | copy-start | bytes 19660804
  461.6 175.1 %all-gather.17.cloned.1.call-start = ((), (), s32[]{:S(2)}) async-start(), calls=%async_computation.9 | async-start | bytes 1179648 | tf_op jit(solution)/shard_map/all_gather | solution.py:66
  582.7 123.3 %all-gather.15.cloned.1.call-start = ((), (), s32[]{:S(2)}) async-start(), calls=%async_computation.8 | async-start | bytes 4325376 | tf_op jit(solution)/shard_map/all_gather | solution.py:65
  710.7 12.5 %copy-start.2 = (f32[100,64,128]{2,1,0:T(8,128)S(1)}, f32[100,64,128]{2,1,0:T(8,128)}, u32[]{:S(2)}) copy-start(f32[100,64,128]{2,1,0:T(8,128)} %gather_fusion.2) | copy-start | bytes 9830404
  710.7 12.5 %copy-start.3 = (f32[100,64,128]{2,1,0:T(8,128)S(1)}, f32[100,64,128]{2,1,0:T(8,128)}, u32[]{:S(2)}) copy-start(f32[100,64,128]{2,1,0:T(8,128)} %gather_fusion.5) | copy-start | bytes 9830404
Sparse Core Ops, SparseCore 0:
  10.0 53.5 all-gather.6
  89.5 121.7 reduce-scatter.2
  213.2 68.5 all-gather.10
  284.3 49.3 all-gather.12
  335.4 67.3 all-gather.8
  461.7 120.8 reduce-scatter.4
  585.3 51.3 all-gather.16
  638.6 67.3 all-gather.14
where the time goes:
time: 760 us; the launch traced here: 751 us
  waiting for transfers between devices  601 us (79%)
  matrix products  101 us (13%)
  local copies, waits for them, and re-layouts  33.3 us (4%)
  between operations  14.1 us (2%)
    reduce_scatter x2, waiting for transfers between devices, shards(): lax.psum_scatter(rows_term(jnp.int32(0), slab_blocks * lax.axis_size('col...  242 us
    all_gather x2, waiting for transfers between devices, shards(): row_totals = lax.all_gather(own_totals, 'col', axis=0, tiled=True)  131 us
    all_gather x2, waiting for transfers between devices, shards(): col_totals = lax.all_gather(own_totals, 'row', axis=0, tiled=True)  101 us
    all_gather x1, waiting for transfers between devices, shards(): row_samples = lax.all_gather(samples, 'col', axis=0, tiled=True)  69.6 us
    all_gather x1, waiting for transfers between devices, shards(): col_samples = lax.all_gather(samples, 'row', axis=0, tiled=True)  54.9 us
    dot_general x2, matrix products, gradient_blocks(): jnp.einsum('snb,snk->sbk', left_samples, right_totals, precision=lax.Prec...  40.1 us
    dot_general x2, matrix products, shards(): jnp.einsum('snk,sbk->snb', picked_cols, current, precision=lax.Precision....  27.8 us
    dot_general x2, matrix products, gradient_blocks(): jnp.einsum('snb,snk->sbk', left_totals, right_samples, precision=lax.Prec...  25 us
  transfers between devices with their start and end apart: 8, of which 8 were waited for; matrix products, arithmetic and copies ran while one was open for 2% of the time, Pallas kernels for 0%

commit v1 on v0

--- a/solution.py
+++ b/solution.py
@@ -43,7 +43,9 @@
     slab_ids = col_ids // slab_blocks
     local_cols = jnp.where(active, slab_ids // col_count * slab_blocks + col_ids % slab_blocks, 0)
     on_diagonal = active & (row_ids == col_ids)
-    row_samples = lax.all_gather(samples, "col", axis=0, tiled=True)
+    row_samples = jnp.concatenate(
+        lax.all_to_all(jnp.stack([samples] * lax.axis_size("col")), "col", 0, 0), axis=0
+    )
     col_samples = lax.all_gather(samples, "row", axis=0, tiled=True)
     picked_cols = col_samples[local_cols]
     picked_rows = row_samples[safe_rows]

time: 760 us -> 715 us (0.941)
  waiting for transfers between devices: 601 us -> 544 us
  starting transfers between devices: 0.49 us -> 9.29 us
    all_to_all x0 -> x1, waiting for transfers between devices: none -> 101 us  [shards(): lax.all_to_all(jnp.stack([samples] * lax.axis_size('col')), 'col', 0, 0)]
    all_gather x1 -> x0, waiting for transfers between devices: 69.6 us -> none  [shards(): row_samples = lax.all_gather(samples, 'col', axis=0, tiled=True)]
    all_gather x2, waiting for transfers between devices: 101 us -> 52.9 us  [shards(): col_totals = lax.all_gather(own_totals, 'row', axis=0, tiled=True)]
    all_gather x2, waiting for transfers between devices: 131 us -> 90.5 us  [shards(): row_totals = lax.all_gather(own_totals, 'col', axis=0, tiled=True)]
    all_to_all x0 -> x1, starting transfers between devices: none -> 9.05 us  [shards(): lax.all_to_all(jnp.stack([samples] * lax.axis_size('col')), 'col', 0, 0)]
  transfers between devices with their start and end apart: 8 -> 8, of which waited for: 8 -> 7; matrix products, arithmetic and copies ran while one was open for 2% -> 2% of each run, Pallas kernels for 0% -> 0%
where the time goes in v1:
time: 715 us; the launch traced here: 706 us
  waiting for transfers between devices  544 us (76%)
  matrix products  101 us (14%)
  local copies, waits for them, and re-layouts  35.9 us (5%)
  between operations  14.1 us (2%)
  starting transfers between devices  9.29 us (1%)
    reduce_scatter x2, waiting for transfers between devices, shards(): lax.psum_scatter(rows_term(jnp.int32(0), slab_blocks * lax.axis_size('col...  243 us
    all_to_all x1, waiting for transfers between devices, shards(): lax.all_to_all(jnp.stack([samples] * lax.axis_size('col')), 'col', 0, 0)  101 us
    all_gather x2, waiting for transfers between devices, shards(): row_totals = lax.all_gather(own_totals, 'col', axis=0, tiled=True)  90.5 us
    all_gather x1, waiting for transfers between devices, shards(): col_samples = lax.all_gather(samples, 'row', axis=0, tiled=True)  54.9 us
    all_gather x2, waiting for transfers between devices, shards(): col_totals = lax.all_gather(own_totals, 'row', axis=0, tiled=True)  52.9 us
    dot_general x2, matrix products, gradient_blocks(): jnp.einsum('snb,snk->sbk', left_samples, right_totals, precision=lax.Prec...  40.1 us
    dot_general x2, matrix products, shards(): jnp.einsum('snk,sbk->snb', picked_cols, current, precision=lax.Precision....  27.8 us
    dot_general x2, matrix products, gradient_blocks(): jnp.einsum('snb,snk->sbk', left_totals, right_samples, precision=lax.Prec...  25 us
  transfers between devices with their start and end apart: 8, of which 7 were waited for; matrix products, arithmetic and copies ran while one was open for 2% of the time, Pallas kernels for 0%

profile of v1, /device:TPU:1, one launch (start us, length us, event | category | flops | bytes accessed | tf_op | source)
XLA Modules:
  0.0 705.8 jit_solution(13332673200302202649)
XLA Ops:
  6.5 0.7 all-gather.6.cloned.1.call-update
  7.3 0.7 fusion.16
  8.0 0.7 bitcast_select_fusion.2
  8.7 54.9 %all-gather.6.cloned.1.call-done = f32[32,64,128]{2,1,0:T(8,128)} async-done(((f32[4,64,128]{2,1,0:T(8,128)}), f32[32,64,128]{2,1,0:T(8,128)}) %all-gather.6.cloned.1.call-update) | async-done | bytes 1048592 | tf_op jit(solution)/shard_map/all_gather | solution.py:49
  63.6 2.0 gather_fusion
  65.6 14.8 %fusion.3 = f32[100,64,128]{2,1,0:T(8,128)S(1)} fusion(f32[100,64,128]{2,1,0:T(8,128)S(1)} %gather_fusion, f32[1,1,100,128,128]{4,3,2,1,0:T(8,128)} %param.5), kind=kOutput, calls=%fused_computation.12 | convolution fusion | flops 1258291200 | bytes 13107200 | tf_op jit(solution)/shard_map/snk,sbk->snb/dot_general | solution.py:53
  80.4 0.4 slice_bitcast_fusion.1
  80.8 4.1 fusion.7
  84.9 4.4 copy.16
  89.4 121.9 %reduce-scatter.3.cloned.1.call-done = f32[4,64,128]{2,1,0:T(8,128)} async-done(((f32[128,64,128]{2,1,0:T(8,128)}), f32[4,64,128]{2,1,0:T(8,128)}) %reduce-scatter.3.cloned.1.call-update) | async-done | bytes 131088 | tf_op jit(solution)/shard_map/reduce_scatter | solution.py:61
  211.4 2.5 stack.2
  213.9 9.0 %all-to-all-start = ((f32[32,4,64,128]{3,2,1,0:T(8,128)}), f32[32,4,64,128]{3,2,1,0:T(8,128)}, u32[]{:S(2)}, u32[]{:S(2)}) async-start(f32[32,4,64,128]{3,2,1,0:T(8,128)} %stack.2), calls=%async_computation.1 | async-start | bytes 8388608 | tf_op jit(solution)/shard_map/all_to_all | solution.py:47
  223.0 0.5 all-gather.8.cloned.1.call-update
  223.7 101.1 %all-to-all-done = f32[32,4,64,128]{3,2,1,0:T(8,128)} async-done(((f32[32,4,64,128]{3,2,1,0:T(8,128)}), f32[32,4,64,128]{3,2,1,0:T(8,128)}, u32[]{:S(2)}, u32[]{:S(2)}) %all-to-all-start) | async-done | bytes 4194336 | tf_op jit(solution)/shard_map/all_to_all | solution.py:47
  324.8 4.6 gather_fusion.2
  329.4 3.6 gather_fusion.3
  333.1 25.0 %all-gather.8.cloned.1.call-done = f32[128,64,128]{2,1,0:T(8,128)} async-done(((f32[4,64,128]{2,1,0:T(8,128)}), f32[128,64,128]{2,1,0:T(8,128)}) %all-gather.8.cloned.1.call-update) | async-done | bytes 4194320 | tf_op jit(solution)/shard_map/all_gather | solution.py:67
  358.1 4.7 gather_fusion.1
  362.7 12.5 %fusion.19 = f32[100,128,128]{2,1,0:T(8,128)S(1)} fusion(f32[100,64,128]{2,1,0:T(8,128)} %gather_fusion.1, f32[100,64,128]{2,1,0:T(8,128)S(1)} %gather_fusion), kind=kOutput, calls=%fused_computation.48 | convolution fusion | flops 1258291200 | bytes 13107200 | tf_op jit(solution)/shard_map/snb,snk->sbk/dot_general | solution.py:12
  375.3 19.4 %fusion = f32[100,128,128]{2,1,0:T(8,128)S(1)} fusion(f32[1,1,100,128,128]{4,3,2,1,0:T(8,128)} %param.5, f32[100,128,128]{2,1,0:T(8,128)S(1)} %fusion.19, pred[100]{0:T(512)(128)(4,1)S(1)} %fusion.18, pred[128,128]{1,0:T(8,128)(4,1)S(1)} %iota_compare_fusion, pred[100]{0:T(512)(128)(4,1)S(1)} %bitcast_and_fusion, f32[100,64,128]{2,1,0:T(8,128)S(1)} %copy-done.1, ...), kind=kOutput, calls=%fused_computation.8 | convolution fusion | flops 1282867200 | bytes 26230984 | tf_op jit(solution)/shard_map/snb,snk->sbk/dot_general | solution.py:15
  394.7 12.9 %fusion.20 = f32[100,64,128]{2,1,0:T(8,128)S(1)} fusion(f32[100,64,128]{2,1,0:T(8,128)S(1)} %gather_fusion, f32[100,128,128]{2,1,0:T(8,128)S(1)} %fusion), kind=kOutput, calls=%fused_computation.49 | convolution fusion | flops 1258291200 | bytes 13107200 | tf_op jit(solution)/shard_map/snk,sbk->snb/dot_general | solution.py:53
  407.6 0.4 slice_bitcast_fusion
  408.0 4.1 fusion.5
  412.1 4.7 copy.18
  416.9 120.7 %reduce-scatter.5.cloned.1.call-done = f32[4,64,128]{2,1,0:T(8,128)} async-done(((f32[128,64,128]{2,1,0:T(8,128)}), f32[4,64,128]{2,1,0:T(8,128)}) %reduce-scatter.5.cloned.1.call-update) | async-done | bytes 131088 | tf_op jit(solution)/shard_map/reduce_scatter | solution.py:61
  537.7 0.7 all-gather.12.cloned.1.call-update
  538.4 52.9 %all-gather.14.cloned.1.call-done = f32[32,64,128]{2,1,0:T(8,128)} async-done(((f32[4,64,128]{2,1,0:T(8,128)}), f32[32,64,128]{2,1,0:T(8,128)}) %all-gather.14.cloned.1.call-update) | async-done | bytes 1048592 | tf_op jit(solution)/shard_map/all_gather | solution.py:68
  591.3 3.7 gather_fusion.5
  595.0 65.5 %all-gather.12.cloned.1.call-done = f32[128,64,128]{2,1,0:T(8,128)} async-done(((f32[4,64,128]{2,1,0:T(8,128)}), f32[128,64,128]{2,1,0:T(8,128)}) %all-gather.12.cloned.1.call-update) | async-done | bytes 4194320 | tf_op jit(solution)/shard_map/all_gather | solution.py:67
  660.6 4.7 gather_fusion.4
  665.3 12.5 %fusion.21 = f32[100,128,128]{2,1,0:T(8,128)S(1)} fusion(f32[100,64,128]{2,1,0:T(8,128)} %gather_fusion.4, f32[100,64,128]{2,1,0:T(8,128)S(1)} %gather_fusion), kind=kOutput, calls=%fused_computation.50 | convolution fusion | flops 1258291200 | bytes 13107200 | tf_op jit(solution)/shard_map/snb,snk->sbk/dot_general | solution.py:12
  677.8 20.7 %fusion.2 = f32[1,1,100,128,128]{4,3,2,1,0:T(8,128)} fusion(f32[100,128,128]{2,1,0:T(8,128)} %copy-done, f32[100,128,128]{2,1,0:T(8,128)S(1)} %fusion.21, pred[100]{0:T(512)(128)(4,1)S(1)} %fusion.18, pred[128,128]{1,0:T(8,128)(4,1)S(1)} %iota_compare_fusion, pred[100]{0:T(512)(128)(4,1)S(1)} %bitcast_and_fusion, f32[100,64,128]{2,1,0:T(8,128)S(1)} %copy-done.2, ...), kind=kOutput, calls=%fused_computation.10 | convolution fusion | flops 1282867200 | bytes 26230984 | tf_op jit(solution)/shard_map/snb,snk->sbk/dot_general | solution.py:15
  (33 shorter events, 0.4 us)
Async XLA Ops:
  6.5 57.0 %all-gather.6.cloned.1.call-start = ((), (), s32[]{:S(2)}) async-start(), calls=%async_computation.3 | async-start | bytes 1179648 | tf_op jit(solution)/shard_map/all_gather | solution.py:49
  7.3 204.1 %reduce-scatter.3.cloned.1.call-start = ((), (), s32[]{:S(2)}) async-start(), calls=%async_computation.4 | async-start | bytes 4325376 | tf_op jit(solution)/shard_map/reduce_scatter | solution.py:61
  89.4 122.0 %copy-start.5 = (f32[4,64,128]{2,1,0:T(8,128)S(1)}, f32[4,64,128]{2,1,0:T(8,128)}, u32[]{:S(2)}) copy-start(f32[4,64,128]{2,1,0:T(8,128)} %param.4) | copy-start | bytes 393220
  89.4 240.0 %all-gather.10.cloned.1.call-start = ((), (), s32[]{:S(2)}) async-start(), calls=%async_computation.6 | async-start | bytes 1179648 | tf_op jit(solution)/shard_map/all_gather | solution.py:68
  213.9 9.7 %copy-start.6 = (s32[1,1,100]{2,1,0:T(1,128)S(1)}, s32[1,1,100]{2,1,0:T(1,128)}, u32[]{:S(2)}) copy-start(s32[1,1,100]{2,1,0:T(1,128)} %param.6) | copy-start | bytes 1204
  213.9 9.7 %copy-start.7 = (s32[1,1,100]{2,1,0:T(1,128)S(1)}, s32[1,1,100]{2,1,0:T(1,128)}, u32[]{:S(2)}) copy-start(s32[1,1,100]{2,1,0:T(1,128)} %param.7) | copy-start | bytes 1204
  213.9 110.9 %all-to-all-start = ((f32[32,4,64,128]{3,2,1,0:T(8,128)}), f32[32,4,64,128]{3,2,1,0:T(8,128)}, u32[]{:S(2)}, u32[]{:S(2)}) async-start(f32[32,4,64,128]{3,2,1,0:T(8,128)} %stack.2), calls=%async_computation.1 | async-start | bytes 8388608 | tf_op jit(solution)/shard_map/all_to_all | solution.py:47
  223.0 135.1 %all-gather.8.cloned.1.call-start = ((), (), s32[]{:S(2)}) async-start(), calls=%async_computation.5 | async-start | bytes 4325376 | tf_op jit(solution)/shard_map/all_gather | solution.py:67
  223.5 314.1 %reduce-scatter.5.cloned.1.call-start = ((), (), s32[]{:S(2)}) async-start(), calls=%async_computation.7 | async-start | bytes 4325376 | tf_op jit(solution)/shard_map/reduce_scatter | solution.py:61
  362.7 12.5 %copy-start.1 = (f32[100,64,128]{2,1,0:T(8,128)S(1)}, f32[100,64,128]{2,1,0:T(8,128)}, u32[]{:S(2)}) copy-start(f32[100,64,128]{2,1,0:T(8,128)} %gather_fusion.2) | copy-start | bytes 9830404
  362.7 12.5 %copy-start.4 = (f32[100,64,128]{2,1,0:T(8,128)S(1)}, f32[100,64,128]{2,1,0:T(8,128)}, u32[]{:S(2)}) copy-start(f32[100,64,128]{2,1,0:T(8,128)} %gather_fusion.3) | copy-start | bytes 9830404
  394.6 13.0 %copy-start = (f32[100,128,128]{2,1,0:T(8,128)}, f32[100,128,128]{2,1,0:T(8,128)S(1)}, u32[]{:S(2)}) copy-start(f32[100,128,128]{2,1,0:T(8,128)S(1)} %fusion) | copy-start | bytes 19660804
  416.9 174.4 %all-gather.14.cloned.1.call-start = ((), (), s32[]{:S(2)}) async-start(), calls=%async_computation.9 | async-start | bytes 1179648 | tf_op jit(solution)/shard_map/all_gather | solution.py:68
  537.7 122.9 %all-gather.12.cloned.1.call-start = ((), (), s32[]{:S(2)}) async-start(), calls=%async_computation.8 | async-start | bytes 4325376 | tf_op jit(solution)/shard_map/all_gather | solution.py:67
  665.3 12.5 %copy-start.2 = (f32[100,64,128]{2,1,0:T(8,128)S(1)}, f32[100,64,128]{2,1,0:T(8,128)}, u32[]{:S(2)}) copy-start(f32[100,64,128]{2,1,0:T(8,128)} %gather_fusion.2) | copy-start | bytes 9830404
  665.3 12.5 %copy-start.3 = (f32[100,64,128]{2,1,0:T(8,128)S(1)}, f32[100,64,128]{2,1,0:T(8,128)}, u32[]{:S(2)}) copy-start(f32[100,64,128]{2,1,0:T(8,128)} %gather_fusion.5) | copy-start | bytes 9830404
Sparse Core Ops, SparseCore 0:
  10.0 53.5 all-gather.5
  89.5 121.7 reduce-scatter.2
  214.0 63.0 all-gather.9
  278.8 79.2 all-gather.7
  417.0 120.5 reduce-scatter.4
  540.1 51.1 all-gather.13
  593.2 67.3 all-gather.11
